TPU v7x, 32 devices: a whole 2x2x4 slice. The times are simulated.
32 devices in a mesh: rep: 8 (over z, x), shard: 4 (over y, core).
Axes of the slice: x: 2, y: 2, z: 4, core: 2. Of those that a mesh axis runs over, the one named last changes fastest.
Arguments:
- latent_tokens: bfloat16 [256, 256, 384], P(('rep', 'shard')), may hold values from -6 to 6
- cond: bfloat16 [256, 384], P(('rep', 'shard')), may hold values from -6 to 6
- w_ada: bfloat16 [384, 2304], P('shard'), may hold values from -0.3125 to 0.3125
- b_ada: bfloat16 [2304], P('shard'), may hold values from -3 to 3
- w_qkv: bfloat16 [384, 1152], P('shard'), may hold values from -0.3125 to 0.3125
- b_qv: bfloat16 [768], P('shard'), may hold values from -3 to 3
- w_o: bfloat16 [384, 384], P('shard'), may hold values from -0.875 to 0.875
- b_o: bfloat16 [384], P('shard'), may hold values from -3 to 3
- w_1: bfloat16 [384, 1536], P('shard'), may hold values from -0.3125 to 0.3125
- b_1: bfloat16 [1536], P('shard'), may hold values from -3 to 3
- w_2: bfloat16 [1536, 384], P('shard'), may hold values from -0.15625 to 0.15625
- b_2: bfloat16 [384], P('shard'), may hold values from -3 to 3
- grad_out: bfloat16 [256, 256, 384], P(('rep', 'shard')), may hold values from -6 to 6
Outputs:
- block_out: bfloat16 [256, 256, 384], P(('rep', 'shard'))
- grad_tokens: float32 [256, 256, 384], P(('rep', 'shard'))
- grad_cond: float32 [256, 384], P(('rep', 'shard'))
- grad_w_ada: float32 [384, 2304], P('shard')
- grad_b_ada: float32 [2304], P('shard')
- grad_w_qkv: float32 [384, 1152], P('shard')
- grad_b_qv: float32 [768], P('shard')
- grad_w_o: float32 [384, 384], P('shard')
- grad_b_o: float32 [384], P('shard')
- grad_w_1: float32 [384, 1536], P('shard')
- grad_b_1: float32 [1536], P('shard')
- grad_w_2: float32 [1536, 384], P('shard')
- grad_b_2: float32 [384], P('shard')
All inputs are finite; a program needn't handle non-finite values.
Results may differ from a plain program's by a relative error of at most 0.019.
The roundings to bfloat16 on the way count: a program that leaves them out, or rounds other values in their place, can miss the bound.
Values may be sent and summed in bfloat16 or wider, within the bound.
No kernel may reach another device: no remote copies, remote signals or barrier semaphores. Data moves between devices by JAX's collectives and lax.ppermute only.
A program may use at most 128 MiB of HBM per device.

v0:
```python
import math
import jax
import jax.numpy as jnp
from jax import lax
from jax.sharding import PartitionSpec as P

HEADS = 6


def layer_norm(value):
    centred = value - jnp.mean(value, axis=-1, keepdims=True)
    factor = lax.rsqrt(jnp.mean(centred * centred, axis=-1, keepdims=True) + 1e-06)
    return (centred * factor, factor)


def norm_back(normed, factor, grad_normed):
    inner = jnp.mean(grad_normed, axis=-1, keepdims=True)
    along = jnp.mean(grad_normed * normed, axis=-1, keepdims=True)
    return factor * (grad_normed - inner - normed * along)


def project(left, right):
    return jnp.einsum("lsd,de->lse", left, right, preferred_element_type=jnp.float32)


def weight_grad(left, right):
    return jnp.einsum("lsd,lse->de", left, right, preferred_element_type=jnp.float32)


def attend(items):
    query, key, value = items
    scores = jnp.einsum("lqhd,lkhd->lhqk", query, key, preferred_element_type=jnp.float32) * 0.125
    top = jnp.max(scores, axis=-1, keepdims=True)
    expo = jnp.exp(scores - top)
    total = jnp.sum(expo, axis=-1, keepdims=True)
    probs = (expo / total).astype(jnp.bfloat16)
    attended = jnp.einsum("lhqk,lkhd->lqhd", probs, value, preferred_element_type=jnp.float32)
    return (attended.astype(jnp.bfloat16), top + jnp.log(total))


def attend_back(items):
    query, key, value, logsum, grad_att = items
    scores = jnp.einsum("lqhd,lkhd->lhqk", query, key, preferred_element_type=jnp.float32) * 0.125
    probs = jnp.exp(scores - logsum)
    rounded = probs.astype(jnp.bfloat16)
    grad_value = jnp.einsum(
        "lhqk,lqhd->lkhd", rounded, grad_att, preferred_element_type=jnp.float32
    )
    grad_probs = jnp.einsum("lqhd,lkhd->lhqk", grad_att, value, preferred_element_type=jnp.float32)
    row_total = jnp.sum(probs * grad_probs, axis=-1, keepdims=True)
    grad_scores = (probs * (grad_probs - row_total)).astype(jnp.bfloat16)
    grad_query = (
        jnp.einsum("lhqk,lkhd->lqhd", grad_scores, key, preferred_element_type=jnp.float32) * 0.125
    )
    grad_key = (
        jnp.einsum("lhqk,lqhd->lkhd", grad_scores, query, preferred_element_type=jnp.float32)
        * 0.125
    )
    return (
        grad_query.astype(jnp.bfloat16),
        grad_key.astype(jnp.bfloat16),
        grad_value.astype(jnp.bfloat16),
    )


def on_device(
    latent_tokens, cond, w_ada, b_ada, w_qkv, b_qv, w_o, b_o, w_1, b_1, w_2, b_2, grad_out
):
    count, length, width = latent_tokens.shape
    head_size = width // HEADS
    per_block = math.gcd(count, max(1, 512 // length))
    blocks = count // per_block
    whole = (
        lax.all_gather(w_ada, "shard", axis=0, tiled=True),
        lax.all_gather(b_ada, "shard", axis=0, tiled=True),
        lax.all_gather(w_qkv, "shard", axis=0, tiled=True),
        lax.all_gather(b_qv, "shard", axis=0, tiled=True),
        lax.all_gather(w_o, "shard", axis=0, tiled=True),
        lax.all_gather(b_o, "shard", axis=0, tiled=True),
        lax.all_gather(w_1, "shard", axis=0, tiled=True),
        lax.all_gather(b_1, "shard", axis=0, tiled=True),
        lax.all_gather(w_2, "shard", axis=0, tiled=True),
        lax.all_gather(b_2, "shard", axis=0, tiled=True),
    )
    f_ada, f_bada, f_qkv, f_bqv, f_wo, f_bo, f_w1, f_b1, f_w2, f_b2 = whole
    tokens = latent_tokens.astype(jnp.float32)
    condition = cond.astype(jnp.float32)
    cs = jax.nn.silu(condition).astype(jnp.bfloat16)
    ada = jnp.dot(cs, f_ada, preferred_element_type=jnp.float32) + f_bada.astype(jnp.float32)
    shift1, scale1, gate1, shift2, scale2, gate2 = jnp.split(ada, 6, axis=-1)
    n1, rstd1 = layer_norm(tokens)
    m1 = (n1 * (1.0 + scale1[:, None]) + shift1[:, None]).astype(jnp.bfloat16)
    qkv = project(m1, f_qkv)
    bias_qv = f_bqv.astype(jnp.float32)
    query = (qkv[..., :width] + bias_qv[:width]).astype(jnp.bfloat16)
    key = qkv[..., width : 2 * width].astype(jnp.bfloat16)
    value = (qkv[..., 2 * width :] + bias_qv[width:]).astype(jnp.bfloat16)
    shape_blocks = (blocks, per_block, length, HEADS, head_size)
    q_blocks = query.reshape(shape_blocks)
    k_blocks = key.reshape(shape_blocks)
    v_blocks = value.reshape(shape_blocks)
    att_blocks, logsum = lax.map(attend, (q_blocks, k_blocks, v_blocks))
    attended = att_blocks.reshape(count, length, width)
    branch = project(attended, f_wo) + f_bo.astype(jnp.float32)
    x1 = tokens + gate1[:, None] * branch
    n2, rstd2 = layer_norm(x1)
    m2 = (n2 * (1.0 + scale2[:, None]) + shift2[:, None]).astype(jnp.bfloat16)
    hidden = project(m2, f_w1) + f_b1.astype(jnp.float32)
    gelu_out, gelu_vjp = jax.vjp(lambda t: jax.nn.gelu(t, approximate=True), hidden)
    gelu_low = gelu_out.astype(jnp.bfloat16)
    ffn = project(gelu_low, f_w2) + f_b2.astype(jnp.float32)
    block_out = (x1 + gate2[:, None] * ffn).astype(jnp.bfloat16)
    again = (
        lax.all_gather(w_ada, "shard", axis=0, tiled=True),
        lax.all_gather(w_qkv, "shard", axis=0, tiled=True),
        lax.all_gather(w_o, "shard", axis=0, tiled=True),
        lax.all_gather(w_1, "shard", axis=0, tiled=True),
        lax.all_gather(w_2, "shard", axis=0, tiled=True),
    )
    g_ada, g_qkv, g_wo, g_w1, g_w2 = again
    cotangent = grad_out.astype(jnp.float32)
    grad_ffn = (cotangent * gate2[:, None]).astype(jnp.bfloat16)
    d_gate2 = jnp.sum(cotangent * ffn, axis=1)
    gw_2 = weight_grad(gelu_low, grad_ffn)
    gb_2 = jnp.sum(grad_ffn.astype(jnp.float32), axis=(0, 1))
    grad_gelu = jnp.einsum("lse,de->lsd", grad_ffn, g_w2, preferred_element_type=jnp.float32)
    grad_hidden = gelu_vjp(grad_gelu)[0].astype(jnp.bfloat16)
    gw_1 = weight_grad(m2, grad_hidden)
    gb_1 = jnp.sum(grad_hidden.astype(jnp.float32), axis=(0, 1))
    grad_m2 = jnp.einsum("lse,de->lsd", grad_hidden, g_w1, preferred_element_type=jnp.float32)
    d_scale2 = jnp.sum(grad_m2 * n2, axis=1)
    d_shift2 = jnp.sum(grad_m2, axis=1)
    grad_x1 = cotangent + norm_back(n2, rstd2, grad_m2 * (1.0 + scale2[:, None]))
    grad_branch = (grad_x1 * gate1[:, None]).astype(jnp.bfloat16)
    d_gate1 = jnp.sum(grad_x1 * branch, axis=1)
    gw_o = weight_grad(attended, grad_branch)
    gb_o = jnp.sum(grad_branch.astype(jnp.float32), axis=(0, 1))
    grad_att = jnp.einsum(
        "lse,de->lsd", grad_branch, g_wo, preferred_element_type=jnp.float32
    ).astype(jnp.bfloat16)
    dq, dk, dv = lax.map(
        attend_back, (q_blocks, k_blocks, v_blocks, logsum, grad_att.reshape(shape_blocks))
    )
    grad_qkv = jnp.concatenate(
        [
            dq.reshape(count, length, width),
            dk.reshape(count, length, width),
            dv.reshape(count, length, width),
        ],
        axis=-1,
    )
    gw_qkv = weight_grad(m1, grad_qkv)
    column_sums = jnp.sum(grad_qkv.astype(jnp.float32), axis=(0, 1))
    gb_qv = jnp.concatenate([column_sums[:width], column_sums[2 * width :]])
    grad_m1 = jnp.einsum("lse,de->lsd", grad_qkv, g_qkv, preferred_element_type=jnp.float32)
    d_scale1 = jnp.sum(grad_m1 * n1, axis=1)
    d_shift1 = jnp.sum(grad_m1, axis=1)
    grad_tokens = grad_x1 + norm_back(n1, rstd1, grad_m1 * (1.0 + scale1[:, None]))
    grad_ada = jnp.concatenate(
        [d_shift1, d_scale1, d_gate1, d_shift2, d_scale2, d_gate2], axis=-1
    ).astype(jnp.bfloat16)
    gw_ada = jnp.dot(cs.T, grad_ada, preferred_element_type=jnp.float32)
    gb_ada = jnp.sum(grad_ada.astype(jnp.float32), axis=0)
    grad_cs = jnp.dot(grad_ada, g_ada.T, preferred_element_type=jnp.float32)
    silu_grad = jax.vjp(jax.nn.silu, condition)[1](grad_cs)[0]
    partial_value = (
        lax.psum_scatter(
            gw_ada.astype(jnp.bfloat16), "shard", scatter_dimension=0, tiled=True
        ).astype(jnp.float32),
        lax.psum_scatter(
            gb_ada.astype(jnp.bfloat16), "shard", scatter_dimension=0, tiled=True
        ).astype(jnp.float32),
        lax.psum_scatter(
            gw_qkv.astype(jnp.bfloat16), "shard", scatter_dimension=0, tiled=True
        ).astype(jnp.float32),
        lax.psum_scatter(
            gb_qv.astype(jnp.bfloat16), "shard", scatter_dimension=0, tiled=True
        ).astype(jnp.float32),
        lax.psum_scatter(
            gw_o.astype(jnp.bfloat16), "shard", scatter_dimension=0, tiled=True
        ).astype(jnp.float32),
        lax.psum_scatter(
            gb_o.astype(jnp.bfloat16), "shard", scatter_dimension=0, tiled=True
        ).astype(jnp.float32),
        lax.psum_scatter(
            gw_1.astype(jnp.bfloat16), "shard", scatter_dimension=0, tiled=True
        ).astype(jnp.float32),
        lax.psum_scatter(
            gb_1.astype(jnp.bfloat16), "shard", scatter_dimension=0, tiled=True
        ).astype(jnp.float32),
        lax.psum_scatter(
            gw_2.astype(jnp.bfloat16), "shard", scatter_dimension=0, tiled=True
        ).astype(jnp.float32),
        lax.psum_scatter(
            gb_2.astype(jnp.bfloat16), "shard", scatter_dimension=0, tiled=True
        ).astype(jnp.float32),
    )
    summed = (
        lax.psum(partial_value[0].astype(jnp.bfloat16), "rep").astype(jnp.float32),
        lax.psum(partial_value[1].astype(jnp.bfloat16), "rep").astype(jnp.float32),
        lax.psum(partial_value[2].astype(jnp.bfloat16), "rep").astype(jnp.float32),
        lax.psum(partial_value[3].astype(jnp.bfloat16), "rep").astype(jnp.float32),
        lax.psum(partial_value[4].astype(jnp.bfloat16), "rep").astype(jnp.float32),
        lax.psum(partial_value[5].astype(jnp.bfloat16), "rep").astype(jnp.float32),
        lax.psum(partial_value[6].astype(jnp.bfloat16), "rep").astype(jnp.float32),
        lax.psum(partial_value[7].astype(jnp.bfloat16), "rep").astype(jnp.float32),
        lax.psum(partial_value[8].astype(jnp.bfloat16), "rep").astype(jnp.float32),
        lax.psum(partial_value[9].astype(jnp.bfloat16), "rep").astype(jnp.float32),
    )
    return (
        block_out,
        grad_tokens,
        silu_grad,
        summed[0],
        summed[1],
        summed[2],
        summed[3],
        summed[4],
        summed[5],
        summed[6],
        summed[7],
        summed[8],
        summed[9],
    )


def solution(mesh):
    in_specs = (
        P(("rep", "shard"), None, None),
        P(("rep", "shard"), None),
        P("shard", None),
        P("shard"),
        P("shard", None),
        P("shard"),
        P("shard", None),
        P("shard"),
        P("shard", None),
        P("shard"),
        P("shard", None),
        P("shard"),
        P(("rep", "shard"), None, None),
    )
    out_specs = (
        P(("rep", "shard"), None, None),
        P(("rep", "shard"), None, None),
        P(("rep", "shard"), None),
        P("shard", None),
        P("shard"),
        P("shard", None),
        P("shard"),
        P("shard", None),
        P("shard"),
        P("shard", None),
        P("shard"),
        P("shard", None),
        P("shard"),
    )
    return jax.shard_map(
        on_device, mesh=mesh, in_specs=in_specs, out_specs=out_specs, check_vma=False
    )
```

profile of v0, /device:TPU:0, one launch (start us, length us, event | category | flops | bytes accessed | tf_op | source)
XLA Modules:
  0.0 425.0 jit_solution(18000375624998559178)
XLA Ops:
  13.5 6.1 %all-gather = bf16[4,1,384]{2,1,0:T(2,128)(2,1)S(1)} all-gather(bf16[1,1,384]{2,1,0:T(2,128)(2,1)S(1)} %reshape.148), channel_id=1, replica_groups=mesh['rep'=8,'shard'=4] {'shard'}, dimensions={0}, use_global_device_ids=true | all-gather | bytes 3840 | tf_op jit(solution)/shard_map/all_gather | solution.py:81
  23.6 12.3 %all-reduce.12 = (bf16[2304]{0:T(1024)(128)(2,1)S(1)}, bf16[768]{0:T(1024)(128)(2,1)S(1)}, bf16[384]{0:T(512)(128)(2,1)S(1)}, bf16[384]{0:T(512)(128)(2,1)S(1)}) all-reduce(bf16[2304]{0:T(1024)(128)(2,1)S(1)} %dynamic-update-slice, bf16[768]{0:T(1024)(128)(2,1)S(1)} %dynamic-update-slice.1, ...), channel_id=1, replica_groups=mesh['rep'=8,'shard'=4] {'shard'}, use_global_device_ids=true, to_apply=%add | all-reduce | flops 3840 | bytes 15360
  39.2 5.9 %all_gather.39 = bf16[384,384]{1,0:T(8,128)(2,1)S(1)} all-gather(bf16[96,384]{1,0:T(8,128)(2,1)S(1)} %copy-done.16), channel_id=1, replica_groups=mesh['rep'=8,'shard'=4] {'shard'}, dimensions={0}, use_global_device_ids=true | all-gather | bytes 368640 | tf_op jit(solution)/shard_map/all_gather | solution.py:78
  45.1 11.3 %all_gather.37 = bf16[384,1152]{1,0:T(8,128)(2,1)S(1)} all-gather(bf16[96,1152]{1,0:T(8,128)(2,1)S(1)} %copy-done.15), channel_id=1, replica_groups=mesh['rep'=8,'shard'=4] {'shard'}, dimensions={0}, use_global_device_ids=true | all-gather | bytes 1105920 | tf_op jit(solution)/shard_map/all_gather | solution.py:76
  59.2 3.0 fusion.98
  67.6 2.6 copy.80
  70.2 2.6 copy.78
  74.2 18.9 %while.26 = (s32[]{:T(128)}, bf16[4,2,256,6,64]{2,4,3,1,0:T(8,128)(2,1)}, f32[4,2,6,256,1]{3,2,1,4,0:T(8,128)S(1)}, bf16[4,2,256,6,64]{2,4,3,1,0:T(8,128)(2,1)},...) while((s32[]{:T(128)}, ...), condition=%wide.region_5.6_spmd, body=%wide.region_2.5_spmd.sunk | while | flops 208598016 | bytes 11122777 | solution.py:102
  81.1 2.5 fusion.152
  85.8 2.5 fusion.152
  93.1 4.6 %fusion.115 = (f32[8,256]{1,0:T(8,128)S(1)}, f32[8,256,384]{2,1,0:T(8,128)S(1)}, f32[8,256,384]{2,1,0:T(8,128)}) fusion(f32[384]{0:T(512)S(1)} %convert_element_type.177, f32[8,384]{1,0:T(8,128)S(1)} %get-tuple-element.197, bf16[8,256,384]{2,1,0:T(8,128)(2,1)S(1)} %copy-done, bf16[8,256,384]{1,2,0:T(8,128)(2,1)} %bitcast.178, ...), kind=kOutput, calls=%fused_computation.164 | convolution fusion | flops 607909888 | bytes 9754112 | tf_op jit(solution)/shard_map/lsd,de->lse/dot_general | solution.py:23
  100.7 11.0 %multiply_convert_fusion.1 = (bf16[8,256,1536]{2,1,0:T(8,128)(2,1)}, f32[8,256,1536]{2,1,0:T(8,128)}) fusion(f32[1536]{0:T(1024)} %reshape.150, bf16[384,1536]{1,0:T(8,128)(2,1)} %all-gather.7.cloned.1.call-done, f32[8,256,384]{2,1,0:T(8,128)} %copy-done.1, f32[8,384]{1,0:T(8,128)} %get-tuple-element.193, f32[8,384]{1,0:T(8,128)} %get-tuple-element.194, ...), kind=kOutput, calls=%fused_computation.69 | convolution fusion | flops 2451308544 | bytes 23246848 | tf_op jit(solution)/shard_map/lsd,de->lse/dot_general | solution.py:23
  111.7 15.0 %fusion.120 = (bf16[1536]{0:T(1024)(128)(2,1)}, bf16[8,256,1536]{2,1,0:T(8,128)(2,1)S(1)}) fusion(f32[8,256,1536]{2,1,0:T(8,128)} %get-tuple-element.206, f32[1536]{0:T(1024)} %reshape.150, bf16[1536,384]{1,0:T(8,128)(2,1)} %all-gather.9.cloned.1.call-done, bf16[8,256,384]{2,1,0:T(8,128)(2,1)} %param.29, f32[8,384]{1,0:T(8,128)} %get-tuple-element.192), kind=kOutput, calls=%fused_computation.169 | convolution fusion | flops 2487482880 | bytes 21648384 | tf_op jit(solution)/shard_map/lse,de->lsd/dot_general | solution.py:126
  126.9 3.6 fusion.92
  133.7 6.0 %fusion.79 = (bf16[8,384]{1,0:T(8,128)(2,1)}, bf16[8,256,384]{2,1,0:T(8,128)(2,1)}, bf16[8,384]{1,0:T(8,128)(2,1)}, f32[8,256]{1,0:T(8,128)S(1)}, f32[8,256]{1,0:T(8,128)S(1)}, /*index=5*/bf16[8,384]{1,0:T(8,128)(2,1)}) fusion(bf16[8,256,384]{2,1,0:T(8,128)(2,1)S(1)} %copy-done.13, f32[384]{0:T(512)S(1)} %copy-done.36, f32[8,256,384]{2,1,0:T(8,128)S(1)} %copy-done.2, ...), kind=kOutput, calls=%fused_computation.94 | convolution fusion | flops 2428488704 | bytes 16985600 | tf_op jit(solution)/shard_map/lsd,de->lse/dot_general | solution.py:23
  139.7 4.1 fusion.114
  146.6 3.7 convolution_convert_fusion.1
  150.4 2.6 copy.82
  157.0 37.3 %while.27 = (s32[]{:T(128)}, bf16[4,2,256,6,64]{2,4,3,1,0:T(8,128)(2,1)}, bf16[4,2,256,6,64]{2,4,3,1,0:T(8,128)(2,1)}, bf16[4,2,256,6,64]{2,4,3,1,0:T(8,128)(2,1...) while((s32[]{:T(128)}, ...), condition=%wide.region_12.13_spmd, body=%wide.region_10.12_spmd.sunk | while | flops 513733632 | bytes 33916044 | solution.py:141
  194.3 2.7 copy.85
  197.1 2.6 copy.83
  201.3 6.2 %fusion.82 = bf16[384,1152]{1,0:T(8,128)(2,1)} fusion(bf16[8,256,384]{2,1,0:T(8,128)(2,1)S(1)} %copy-done, f32[8,384]{1,0:T(8,128)S(1)} %copy-done.24, f32[8,384]{1,0:T(8,128)S(1)} %get-tuple-element.196, f32[8,256]{1,0:T(8,128)S(1)} %add_rsqrt_fusion.1, f32[8,256]{1,0:T(8,128)S(1)} %broadcast_multiply_fusion.5, bf16[8,256,384]{2,1,0:T(8,128)(2,1)} %copy.85, ...), kind=kOutput, calls=%fused_computation.111 | convolution fusion | flops 1831256064 | bytes 7217152 | tf_op jit(solution)/shard_map/lsd,lse->de/dot_general | solution.py:27
  207.6 7.6 %fusion.83 = bf16[384,1536]{1,0:T(8,128)(2,1)} fusion(bf16[8,256,1536]{2,1,0:T(8,128)(2,1)} %copy-done.39, f32[8,256,384]{2,1,0:T(8,128)} %copy-done.1, f32[8,384]{1,0:T(8,128)S(1)} %copy-done.29, f32[8,384]{1,0:T(8,128)S(1)} %copy-done.22, f32[8,256]{1,0:T(8,128)S(1)} %copy-done.26, f32[8,256]{1,0:T(8,128)S(1)} %broadcast_multiply_fusion.4), kind=kOutput, calls=%fused_computation.112 | convolution fusion | flops 2420441088 | bytes 10657792 | tf_op jit(solution)/shard_map/lsd,lse->de/dot_general | solution.py:27
  215.5 8.0 %fusion.84 = bf16[1536,384]{1,0:T(8,128)(2,1)} fusion(bf16[8,256,1536]{2,1,0:T(8,128)(2,1)} %get-tuple-element.205, bf16[8,256,384]{2,1,0:T(8,128)(2,1)} %param.29, f32[8,384]{1,0:T(8,128)S(1)} %copy-done.20), kind=kOutput, calls=%fused_computation.113 | convolution fusion | flops 2418868224 | bytes 9056256 | tf_op jit(solution)/shard_map/lsd,lse->de/dot_general | solution.py:27
  223.6 6.2 %fusion.76 = (bf16[8,384]{1,0:T(8,128)(2,1)S(1)}, f32[8,256]{1,0:T(8,128)S(1)}, f32[8,256]{1,0:T(8,128)S(1)}, bf16[8,384]{1,0:T(8,128)(2,1)S(1)}, f32[8,256,384]{2,1,0:T(8,128)S(1)}) fusion(bf16[8,256,384]{2,1,0:T(8,128)(2,1)S(1)} %copy-done, f32[8,256]{1,0:T(8,128)S(1)} %add_rsqrt_fusion.1, f32[8,256]{1,0:T(8,128)S(1)} %broadcast_multiply_fusion.5, ...), kind=kOutput, calls=%fused_computation.91 | convolution fusion | flops 1833949184 | bytes 10379264 | tf_op jit(solution)/shard_map/lse,de->lsd/dot_general | solution.py:155
  229.9 3.1 multiply_reduce_fusion.3
  235.2 24.6 %reduce-scatter.12.cloned.1.call-done = bf16[96,1536]{1,0:T(8,128)(2,1)} async-done(((bf16[384,1536]{1,0:T(8,128)(2,1)}), bf16[96,1536]{1,0:T(8,128)(2,1)}) %reduce-scatter.12.cloned.1.call-update) | async-done | bytes 294928 | tf_op jit(solution)/shard_map/reduce_scatter | solution.py:185
  259.8 28.5 %reduce-scatter.14.cloned.1.call-done = bf16[384,384]{1,0:T(8,128)(2,1)} async-done(((bf16[1536,384]{1,0:T(8,128)(2,1)}), bf16[384,384]{1,0:T(8,128)(2,1)}) %reduce-scatter.14.cloned.1.call-update) | async-done | bytes 294928 | tf_op jit(solution)/shard_map/reduce_scatter | solution.py:191
  288.3 32.0 %reduce-scatter.6.cloned.1.call-done = bf16[96,2304]{1,0:T(8,128)(2,1)} async-done(((bf16[384,2304]{1,0:T(8,128)(2,1)}), bf16[96,2304]{1,0:T(8,128)(2,1)}) %reduce-scatter.6.cloned.1.call-update) | async-done | bytes 442384 | tf_op jit(solution)/shard_map/reduce_scatter | solution.py:167
  325.2 10.5 %all-reduce.11 = (bf16[2304]{0:T(1024)(128)(2,1)S(1)}, bf16[768]{0:T(1024)(128)(2,1)S(1)}, bf16[384]{0:T(512)(128)(2,1)S(1)}, bf16[1536]{0:T(1024)(128)(2,1)S(1)}, bf16[384]{0:T(512)(128)(2,1)S(1)}) all-reduce(bf16[2304]{0:T(1024)(128)(2,1)S(1)} %reduce_sum.215, ...), channel_id=3, replica_groups=mesh['rep'=8,'shard'=4] {'shard'}, use_global_device_ids=true, to_apply=%region_24.25.clone | all-reduce | flops 5376 | bytes 21504
  336.1 22.2 %all-reduce.9 = (bf16[576]{0:T(1024)(128)(2,1)S(1)}, bf16[192]{0:T(256)(128)(2,1)S(1)}, bf16[96]{0:T(256)(128)(2,1)S(1)}, bf16[384]{0:T(512)(128)(2,1)S(1)}, bf16[96]{0:T(256)(128)(2,1)S(1)}) all-reduce(bf16[576]{0:T(1024)(128)(2,1)S(1)} %dynamic-slice.5, ...), channel_id=1, replica_groups=mesh['rep'=8,'shard'=4] {'rep'}, use_global_device_ids=true, to_apply=%region_25.26 | all-reduce | flops 1344 | bytes 5376 | tf_op jit(solution)/shard_map/psum | solution.py:200
  362.3 47.9 %all-reduce.15.cloned.1.call-done = (bf16[96,2304]{1,0:T(8,128)(2,1)}, bf16[96,1152]{1,0:T(8,128)(2,1)}, bf16[96,384]{1,0:T(8,128)(2,1)}, bf16[96,1536]{1,0:T(8,128)(2,1)}, bf16[384,384]{1,0:T(8,128)(2,1)}) async-done(((bf16[96,2304]{1,0:T(8,128)(2,1)}, bf16[96,1152]{1,0:T(8,128)(2,1)}, bf16[96,384]{1,0:T(8,128)(2,1)}, bf16[96,1536]{1,0:T(8,128)(2,1)}, bf16[384,384]{1,0:T(8,128)(2,1)}), ...) | async-done | bytes 1327120 | tf_op jit(solution)/shard_map/psum | solution.py:199
  (218 shorter events, 103.9 us)
Async XLA Ops:
  7.2 31.1 %copy-start = (bf16[8,256,384]{2,1,0:T(8,128)(2,1)S(1)}, bf16[8,256,384]{2,1,0:T(8,128)(2,1)}, u32[]{:S(2)}) copy-start(bf16[8,256,384]{2,1,0:T(8,128)(2,1)} %param.17) | copy-start | bytes 4718596
  7.2 32.0 %copy-start.16 = (bf16[96,384]{1,0:T(8,128)(2,1)S(1)}, bf16[96,384]{1,0:T(8,128)(2,1)}, u32[]{:S(2)}) copy-start(bf16[96,384]{1,0:T(8,128)(2,1)} %param.23) | copy-start | bytes 221188
  7.2 37.9 %copy-start.15 = (bf16[96,1152]{1,0:T(8,128)(2,1)S(1)}, bf16[96,1152]{1,0:T(8,128)(2,1)}, u32[]{:S(2)}) copy-start(bf16[96,1152]{1,0:T(8,128)(2,1)} %param.21) | copy-start | bytes 663556
  7.2 49.2 %copy-start.17 = (bf16[8,384]{1,0:T(8,128)(2,1)S(1)}, bf16[8,384]{1,0:T(8,128)(2,1)}, u32[]{:S(2)}) copy-start(bf16[8,384]{1,0:T(8,128)(2,1)} %param.18) | copy-start | bytes 18436
  7.2 49.2 %all-gather.5.cloned.1.call-start = ((), (), s32[]{:S(2)}) async-start(), calls=%async_computation.5 | async-start | bytes 2211840 | tf_op jit(solution)/shard_map/all_gather | solution.py:74
  8.0 92.7 %all-gather.7.cloned.1.call-start = ((), (), s32[]{:S(2)}) async-start(), calls=%async_computation.6 | async-start | bytes 1474560 | tf_op jit(solution)/shard_map/all_gather | solution.py:80
  8.7 103.0 %all-gather.9.cloned.1.call-start = ((), (), s32[]{:S(2)}) async-start(), calls=%async_computation.7 | async-start | bytes 1474560 | tf_op jit(solution)/shard_map/all_gather | solution.py:82
  9.4 225.7 %reduce-scatter.10.cloned.1.call-start = ((), (), s32[]{:S(2)}) async-start(), calls=%async_computation.10 | async-start | bytes 368640 | tf_op jit(solution)/shard_map/reduce_scatter | solution.py:179
  35.9 57.2 %copy-start.27 = (f32[384]{0:T(512)}, f32[384]{0:T(512)S(1)}, u32[]{:S(2)}) copy-start(f32[384]{0:T(512)S(1)} %convert_element_type.177) | copy-start | bytes 4612
  56.4 5.8 %copy-start.12 = (bf16[384,1152]{1,0:T(8,128)(2,1)}, bf16[384,1152]{1,0:T(8,128)(2,1)S(1)}, u32[]{:S(2)}) copy-start(bf16[384,1152]{1,0:T(8,128)(2,1)S(1)} %all_gather.37) | copy-start | bytes 2654212
  111.7 15.1 %copy-start.38 = (bf16[384,1536]{1,0:T(8,128)(2,1)S(1)}, bf16[384,1536]{1,0:T(8,128)(2,1)}, u32[]{:S(2)}) copy-start(bf16[384,1536]{1,0:T(8,128)(2,1)} %all-gather.7.cloned.1.call-done) | copy-start | bytes 3538948
  126.8 6.8 %copy-start.40 = (bf16[8,256,1536]{2,1,0:T(8,128)(2,1)S(1)}, bf16[8,256,1536]{2,1,0:T(8,128)(2,1)}, u32[]{:S(2)}) copy-start(bf16[8,256,1536]{2,1,0:T(8,128)(2,1)} %get-tuple-element.205) | copy-start | bytes 18874372
  150.3 84.8 %reduce-scatter.8.cloned.1.call-start = ((), (), s32[]{:S(2)}) async-start(), calls=%async_computation.9 | async-start | bytes 1105920 | tf_op jit(solution)/shard_map/reduce_scatter | solution.py:173
  194.3 5.3 %copy-start.8 = (bf16[4,2,256,6,64]{2,4,3,1,0:T(8,128)(2,1)S(1)}, bf16[4,2,256,6,64]{2,4,3,1,0:T(8,128)(2,1)}, u32[]{:S(2)}) copy-start(bf16[4,2,256,6,64]{2,4,3,1,0:T(8,128)(2,1)} %get-tuple-element.98) | copy-start | bytes 4718596
  201.3 6.3 %copy-start.22 = (f32[8,384]{1,0:T(8,128)S(1)}, f32[8,384]{1,0:T(8,128)}, u32[]{:S(2)}) copy-start(f32[8,384]{1,0:T(8,128)} %get-tuple-element.194) | copy-start | bytes 36868
  201.3 6.3 %copy-start.26 = (f32[8,256]{1,0:T(8,128)S(1)}, f32[8,256]{1,0:T(8,128)}, u32[]{:S(2)}) copy-start(f32[8,256]{1,0:T(8,128)} %add_rsqrt_fusion) | copy-start | bytes 24580
  201.3 6.3 %copy-start.29 = (f32[8,384]{1,0:T(8,128)S(1)}, f32[8,384]{1,0:T(8,128)}, u32[]{:S(2)}) copy-start(f32[8,384]{1,0:T(8,128)} %get-tuple-element.193) | copy-start | bytes 36868
  207.5 8.0 %copy-start.20 = (f32[8,384]{1,0:T(8,128)S(1)}, f32[8,384]{1,0:T(8,128)}, u32[]{:S(2)}) copy-start(f32[8,384]{1,0:T(8,128)} %get-tuple-element.192) | copy-start | bytes 36868
  207.5 52.3 %reduce-scatter.12.cloned.1.call-start = ((), (), s32[]{:S(2)}) async-start(), calls=%async_computation.11 | async-start | bytes 1474560 | tf_op jit(solution)/shard_map/reduce_scatter | solution.py:185
  215.2 8.3 %copy-start.10 = (bf16[8,256,384]{2,1,0:T(8,128)(2,1)S(1)}, bf16[8,256,384]{2,1,0:T(8,128)(2,1)}, u32[]{:S(2)}) copy-start(bf16[8,256,384]{2,1,0:T(8,128)(2,1)} %copy.85) | copy-start | bytes 4718596
  215.2 73.0 %reduce-scatter.14.cloned.1.call-start = ((), (), s32[]{:S(2)}) async-start(), calls=%async_computation.12 | async-start | bytes 1474560 | tf_op jit(solution)/shard_map/reduce_scatter | solution.py:191
  223.5 6.3 %copy-start.28 = (f32[384]{0:T(512)S(1)}, f32[384]{0:T(512)}, u32[]{:S(2)}) copy-start(f32[384]{0:T(512)} %copy-done.27) | copy-start | bytes 4612
  223.5 96.8 %reduce-scatter.6.cloned.1.call-start = ((), (), s32[]{:S(2)}) async-start(), calls=%async_computation.8 | async-start | bytes 2211840 | tf_op jit(solution)/shard_map/reduce_scatter | solution.py:167
  223.6 6.2 %copy-start.4 = (f32[8,256,384]{2,1,0:T(8,128)S(1)}, f32[8,256,384]{2,1,0:T(8,128)}, u32[]{:S(2)}) copy-start(f32[8,256,384]{2,1,0:T(8,128)} %get-tuple-element.204) | copy-start | bytes 9437188
  223.6 6.2 %copy-start.5 = (f32[8,256,384]{2,1,0:T(8,128)S(1)}, f32[8,256,384]{2,1,0:T(8,128)}, u32[]{:S(2)}) copy-start(f32[8,256,384]{2,1,0:T(8,128)} %get-tuple-element.174) | copy-start | bytes 9437188
  233.0 89.9 %copy-start.11 = (bf16[8,256,384]{2,1,0:T(8,128)(2,1)S(1)}, bf16[8,256,384]{2,1,0:T(8,128)(2,1)}, u32[]{:S(2)}) copy-start(bf16[8,256,384]{2,1,0:T(8,128)(2,1)} %copy.85) | copy-start | bytes 4718596
  235.0 90.2 %copy-start.33 = (bf16[384]{0:T(512)(128)(2,1)S(1)}, bf16[384]{0:T(512)(128)(2,1)}, u32[]{:S(2)}) copy-start(bf16[384]{0:T(512)(128)(2,1)} %get-tuple-element.172) | copy-start | bytes 2308
  235.0 90.2 %copy-start.34 = (bf16[384]{0:T(512)(128)(2,1)S(1)}, bf16[384]{0:T(512)(128)(2,1)}, u32[]{:S(2)}) copy-start(bf16[384]{0:T(512)(128)(2,1)} %get-tuple-element.191) | copy-start | bytes 2308
  235.0 90.2 %copy-start.35 = (bf16[1536]{0:T(1024)(128)(2,1)S(1)}, bf16[1536]{0:T(1024)(128)(2,1)}, u32[]{:S(2)}) copy-start(bf16[1536]{0:T(1024)(128)(2,1)} %get-tuple-element.208) | copy-start | bytes 9220
  235.0 126.1 %copy-start.6 = (bf16[384,2304]{1,0:T(8,128)(2,1)S(1)}, bf16[384,2304]{1,0:T(8,128)(2,1)}, u32[]{:S(2)}) copy-start(bf16[384,2304]{1,0:T(8,128)(2,1)} %all-gather.5.cloned.1.call-done) | copy-start | bytes 5308420
  235.1 175.2 %all-reduce.15.cloned.1.call-start = ((), (), s32[]{:S(2)}) async-start(), calls=%async_computation.13 | async-start | bytes 2654208 | tf_op jit(solution)/shard_map/psum | solution.py:199
  410.2 7.1 %copy-start.14 = (bf16[384,384]{1,0:T(8,128)(2,1)S(1)}, bf16[384,384]{1,0:T(8,128)(2,1)}, u32[]{:S(2)}) copy-start(bf16[384,384]{1,0:T(8,128)(2,1)} %get-tuple-element.162) | copy-start | bytes 884740
  (21 other events, 71.0 us)
Sparse Core Ops, SparseCore 0:
  9.6 23.5 all-gather.4
  34.8 19.2 all-gather.6
  55.6 17.1 all-gather.8
  150.4 20.4 reduce-scatter.9
  207.6 23.9 reduce-scatter.7
  234.0 25.7 reduce-scatter.11
  262.5 25.7 reduce-scatter.13
  290.9 29.3 reduce-scatter.5
  324.8 85.3 all-reduce.14
where the time goes:
time: 429 us; the launch traced here: 425 us
  waiting for transfers between devices  135 us (31%)
  matrix products  133 us (31%)
  blocking collectives  68.3 us (16%)
  local copies, waits for them, and re-layouts  35.9 us (8%)
  other arithmetic  33 us (8%)
  between operations  19.2 us (4%)
    psum x1, waiting for transfers between devices, on_device(): lax.psum(partial_value[0].astype(jnp.bfloat16), 'rep').astype(jnp.float32)  47.9 us
    reduce_scatter x1, waiting for transfers between devices, on_device(): lax.psum_scatter(gw_ada.astype(jnp.bfloat16), 'shard', scatter_dimension=...  32 us
    reduce_scatter x1, waiting for transfers between devices, on_device(): lax.psum_scatter(gw_2.astype(jnp.bfloat16), 'shard', scatter_dimension=0,...  28.5 us
    dot_general x4, matrix products, project(): jnp.einsum('lsd,de->lse', left, right, preferred_element_type=jnp.float32)  24.6 us
    reduce_scatter x1, waiting for transfers between devices, on_device(): lax.psum_scatter(gw_1.astype(jnp.bfloat16), 'shard', scatter_dimension=0,...  24.6 us
    dot_general x4, matrix products, weight_grad(): jnp.einsum('lsd,lse->de', left, right, preferred_element_type=jnp.float32)  23.4 us
    unnamed x2, blocking collectives  22.9 us
    psum x1, blocking collectives, on_device(): lax.psum(partial_value[1].astype(jnp.bfloat16), 'rep').astype(jnp.float32)  22.2 us
  transfers between devices with their start and end apart: 9, of which 4 were waited for; matrix products, arithmetic and copies ran while one was open for 36% of the time, Pallas kernels for 0%

commit v1 on v0

--- a/solution.py
+++ b/solution.py
@@ -5,6 +5,27 @@
 from jax.sharding import PartitionSpec as P
 
 HEADS = 6
+
+
+def laid_out(blocks, dim):
+    blocks = jnp.moveaxis(blocks, 0, dim)
+    dims = blocks.shape
+    return blocks.reshape(*dims[:dim], dims[dim] * dims[dim + 1], *dims[dim + 2 :])
+
+
+def grow_blocks(shard, axis):
+    size, here = (lax.axis_size(axis), lax.axis_index(axis))
+    blocks, stride = (shard[None], 1)
+    while stride < size:
+        other = lax.ppermute(blocks, axis, [(i, i ^ stride) for i in range(size)])
+        low = here & stride == 0
+        blocks = jnp.concatenate([jnp.where(low, blocks, other), jnp.where(low, other, blocks)])
+        stride *= 2
+    return blocks
+
+
+def collect(value, axis, dim):
+    return laid_out(grow_blocks(value, axis), dim)
 
 
 def layer_norm(value):
@@ -73,7 +94,7 @@
     whole = (
         lax.all_gather(w_ada, "shard", axis=0, tiled=True),
         lax.all_gather(b_ada, "shard", axis=0, tiled=True),
-        lax.all_gather(w_qkv, "shard", axis=0, tiled=True),
+        collect(w_qkv, "shard", 0),
         lax.all_gather(b_qv, "shard", axis=0, tiled=True),
         lax.all_gather(w_o, "shard", axis=0, tiled=True),
         lax.all_gather(b_o, "shard", axis=0, tiled=True),

time: 429 us -> 452 us (1.054)
  waiting for transfers between devices: 135 us -> 157 us
    ppermute x0 -> x2, waiting for transfers between devices: none -> 13.6 us  [grow_blocks(): other = lax.ppermute(blocks, axis, [(i, i ^ stride) for i in range(size)])]
    reduce_scatter x1, waiting for transfers between devices: 0.02 us -> 4.84 us  [on_device(): lax.psum_scatter(gw_qkv.astype(jnp.bfloat16), 'shard', scatter_dimension=...]
    unnamed x100 -> x94, local copies, waits for them, and re-layouts: 12 us -> 10.8 us
  transfers between devices with their start and end apart: 9 -> 11, of which waited for: 4 -> 6; matrix products, arithmetic and copies ran while one was open for 36% -> 23% of each run, Pallas kernels for 0% -> 0%
where the time goes in v1:
time: 452 us; the launch traced here: 445 us
  waiting for transfers between devices  157 us (35%)
  matrix products  131 us (29%)
  blocking collectives  68.7 us (15%)
  local copies, waits for them, and re-layouts  35 us (8%)
  other arithmetic  32 us (7%)
  between operations  19.4 us (4%)
    psum x1, waiting for transfers between devices, on_device(): lax.psum(partial_value[0].astype(jnp.bfloat16), 'rep').astype(jnp.float32)  47.9 us
    reduce_scatter x1, waiting for transfers between devices, on_device(): lax.psum_scatter(gw_ada.astype(jnp.bfloat16), 'shard', scatter_dimension=...  32 us
    reduce_scatter x1, waiting for transfers between devices, on_device(): lax.psum_scatter(gw_2.astype(jnp.bfloat16), 'shard', scatter_dimension=0,...  28.5 us
    reduce_scatter x1, waiting for transfers between devices, on_device(): lax.psum_scatter(gw_1.astype(jnp.bfloat16), 'shard', scatter_dimension=0,...  28.1 us
    dot_general x4, matrix products, project(): jnp.einsum('lsd,de->lse', left, right, preferred_element_type=jnp.float32)  24.7 us
    unnamed x2, blocking collectives  23.9 us
    dot_general x4, matrix products, weight_grad(): jnp.einsum('lsd,lse->de', left, right, preferred_element_type=jnp.float32)  23.8 us
    psum x1, blocking collectives, on_device(): lax.psum(partial_value[1].astype(jnp.bfloat16), 'rep').astype(jnp.float32)  22.2 us
  transfers between devices with their start and end apart: 11, of which 6 were waited for; matrix products, arithmetic and copies ran while one was open for 23% of the time, Pallas kernels for 0%

profile of v1, /device:TPU:0, one launch (start us, length us, event | category | flops | bytes accessed | tf_op | source)
XLA Modules:
  0.0 444.6 jit_solution(3806950361475571462)
XLA Ops:
  16.2 13.4 %all-reduce.12 = (bf16[2304]{0:T(1024)(128)(2,1)S(1)}, bf16[768]{0:T(1024)(128)(2,1)S(1)}, bf16[384]{0:T(512)(128)(2,1)S(1)}, bf16[384]{0:T(512)(128)(2,1)S(1)}) all-reduce(bf16[2304]{0:T(1024)(128)(2,1)S(1)} %dynamic-update-slice, bf16[768]{0:T(1024)(128)(2,1)S(1)} %dynamic-update-slice.1, ...), channel_id=1, replica_groups=mesh['rep'=8,'shard'=4] {'shard'}, use_global_device_ids=true, to_apply=%add | all-reduce | flops 3840 | bytes 15360
  31.4 6.1 %all_gather.37 = bf16[384,384]{1,0:T(8,128)(2,1)S(1)} all-gather(bf16[96,384]{1,0:T(8,128)(2,1)} %param.23), channel_id=1, replica_groups=mesh['rep'=8,'shard'=4] {'shard'}, dimensions={0}, use_global_device_ids=true | all-gather | bytes 368640 | tf_op jit(solution)/shard_map/all_gather | solution.py:99
  38.2 5.1 %all-gather = bf16[4,1,384]{2,1,0:T(2,128)(2,1)S(1)} all-gather(bf16[1,1,384]{2,1,0:T(2,128)(2,1)S(1)} %reshape.152), channel_id=1, replica_groups=mesh['rep'=8,'shard'=4] {'shard'}, dimensions={0}, use_global_device_ids=true | all-gather | bytes 3840 | tf_op jit(solution)/shard_map/all_gather | solution.py:102
  46.8 13.6 %collective-permute-done.1 = bf16[2,96,1152]{2,1,0:T(8,128)(2,1)S(1)} collective-permute-done((bf16[2,96,1152]{2,1,0:T(8,128)(2,1)S(1)}, bf16[2,96,1152]{2,1,0:T(8,128)(2,1)S(1)}, u32[]{:S(2)}, u32[]{:S(2)}) %collective-permute-start.1) | collective-permute-done | bytes 442400 | tf_op jit(solution)/shard_map/ppermute | solution.py:20
  63.1 3.0 fusion.99
  73.2 2.6 copy.80
  77.1 18.9 %while.26 = (s32[]{:T(128)}, bf16[4,2,256,6,64]{2,4,3,1,0:T(8,128)(2,1)}, f32[4,2,6,256,1]{3,2,1,4,0:T(8,128)S(1)}, bf16[4,2,256,6,64]{2,4,3,1,0:T(8,128)(2,1)},...) while((s32[]{:T(128)}, ...), condition=%wide.region_5.6_spmd, body=%wide.region_2.5_spmd.sunk | while | flops 208598016 | bytes 11122769 | solution.py:123
  84.0 2.5 fusion.152
  96.0 4.6 %fusion.114 = (f32[8,256]{1,0:T(8,128)S(1)}, f32[8,256,384]{2,1,0:T(8,128)S(1)}, f32[8,256,384]{2,1,0:T(8,128)}) fusion(f32[384]{0:T(512)S(1)} %convert_element_type.177, f32[8,384]{1,0:T(8,128)S(1)} %get-tuple-element.201, bf16[8,256,384]{2,1,0:T(8,128)(2,1)S(1)} %copy-done, bf16[8,256,384]{1,2,0:T(8,128)(2,1)} %bitcast.25, ...), kind=kOutput, calls=%fused_computation.169 | convolution fusion | flops 607909888 | bytes 9754112 | tf_op jit(solution)/shard_map/lsd,de->lse/dot_general | solution.py:44
  103.6 11.0 %multiply_convert_fusion.1 = (bf16[8,256,1536]{2,1,0:T(8,128)(2,1)}, f32[8,256,1536]{2,1,0:T(8,128)}) fusion(f32[1536]{0:T(1024)} %reshape.154, bf16[384,1536]{1,0:T(8,128)(2,1)} %all-gather.7.cloned.1.call-done, f32[8,256,384]{2,1,0:T(8,128)} %copy-done.1, f32[8,384]{1,0:T(8,128)} %get-tuple-element.197, f32[8,384]{1,0:T(8,128)} %get-tuple-element.198, ...), kind=kOutput, calls=%fused_computation.69 | convolution fusion | flops 2451308544 | bytes 23246848 | tf_op jit(solution)/shard_map/lsd,de->lse/dot_general | solution.py:44
  114.7 14.8 %fusion.119 = (bf16[1536]{0:T(1024)(128)(2,1)}, bf16[8,256,1536]{2,1,0:T(8,128)(2,1)S(1)}) fusion(f32[8,256,1536]{2,1,0:T(8,128)} %get-tuple-element.210, f32[1536]{0:T(1024)} %reshape.154, bf16[1536,384]{1,0:T(8,128)(2,1)} %all-gather.9.cloned.1.call-done, bf16[8,256,384]{2,1,0:T(8,128)(2,1)} %param.29, f32[8,384]{1,0:T(8,128)} %get-tuple-element.196), kind=kOutput, calls=%fused_computation.174 | convolution fusion | flops 2487482880 | bytes 21648384 | tf_op jit(solution)/shard_map/lse,de->lsd/dot_general | solution.py:147
  129.5 3.6 fusion.92
  136.3 6.0 %fusion.79 = (bf16[8,384]{1,0:T(8,128)(2,1)}, bf16[8,256,384]{2,1,0:T(8,128)(2,1)}, bf16[8,384]{1,0:T(8,128)(2,1)}, f32[8,256]{1,0:T(8,128)S(1)}, f32[8,256]{1,0:T(8,128)S(1)}, /*index=5*/bf16[8,384]{1,0:T(8,128)(2,1)}) fusion(bf16[8,256,384]{2,1,0:T(8,128)(2,1)S(1)} %copy-done.9, f32[384]{0:T(512)S(1)} %copy-done.33, f32[8,256,384]{2,1,0:T(8,128)S(1)} %copy-done.2, ...), kind=kOutput, calls=%fused_computation.94 | convolution fusion | flops 2428488704 | bytes 16985600 | tf_op jit(solution)/shard_map/lsd,de->lse/dot_general | solution.py:44
  142.4 4.1 fusion.113
  148.7 3.1 fusion.85
  151.8 2.6 copy.82
  158.5 37.4 %while.27 = (s32[]{:T(128)}, bf16[4,2,256,6,64]{2,4,3,1,0:T(8,128)(2,1)}, bf16[4,2,256,6,64]{2,4,3,1,0:T(8,128)(2,1)}, bf16[4,2,256,6,64]{2,4,3,1,0:T(8,128)(2,1...) while((s32[]{:T(128)}, ...), condition=%wide.region_12.13_spmd, body=%wide.region_10.12_spmd.sunk | while | flops 513733632 | bytes 33916036 | solution.py:162
  195.9 2.8 copy.83
  200.2 2.7 copy.85
  203.1 5.3 %fusion.82 = bf16[384,1152]{1,0:T(8,128)(2,1)} fusion(bf16[8,256,384]{2,1,0:T(8,128)(2,1)S(1)} %copy-done, f32[8,384]{1,0:T(8,128)S(1)} %copy-done.20, f32[8,384]{1,0:T(8,128)S(1)} %get-tuple-element.200, f32[8,256]{1,0:T(8,128)S(1)} %add_rsqrt_fusion.1, f32[8,256]{1,0:T(8,128)S(1)} %broadcast_multiply_fusion.5, bf16[8,256,384]{2,1,0:T(8,128)(2,1)} %copy.85, ...), kind=kOutput, calls=%fused_computation.111 | convolution fusion | flops 1831256064 | bytes 7217152 | tf_op jit(solution)/shard_map/lsd,lse->de/dot_general | solution.py:48
  208.5 7.7 %fusion.83 = bf16[384,1536]{1,0:T(8,128)(2,1)} fusion(bf16[8,256,1536]{2,1,0:T(8,128)(2,1)} %copy-done.36, f32[8,256,384]{2,1,0:T(8,128)} %copy-done.1, f32[8,384]{1,0:T(8,128)S(1)} %copy-done.25, f32[8,384]{1,0:T(8,128)S(1)} %copy-done.18, f32[8,256]{1,0:T(8,128)S(1)} %copy-done.22, f32[8,256]{1,0:T(8,128)S(1)} %broadcast_multiply_fusion.4), kind=kOutput, calls=%fused_computation.112 | convolution fusion | flops 2420441088 | bytes 10657792 | tf_op jit(solution)/shard_map/lsd,lse->de/dot_general | solution.py:48
  216.2 11.4 %all_gather.43 = bf16[384,1152]{1,0:T(8,128)(2,1)} all-gather(bf16[96,1152]{1,0:T(8,128)(2,1)} %param.21), channel_id=1, replica_groups=mesh['rep'=8,'shard'=4] {'shard'}, dimensions={0}, use_global_device_ids=true | all-gather | bytes 1105920 | tf_op jit(solution)/shard_map/all_gather | solution.py:136
  227.6 7.7 %fusion.84 = bf16[1536,384]{1,0:T(8,128)(2,1)} fusion(bf16[8,256,1536]{2,1,0:T(8,128)(2,1)} %get-tuple-element.209, bf16[8,256,384]{2,1,0:T(8,128)(2,1)} %param.29, f32[8,384]{1,0:T(8,128)S(1)} %copy-done.16), kind=kOutput, calls=%fused_computation.113 | convolution fusion | flops 2418868224 | bytes 9056256 | tf_op jit(solution)/shard_map/lsd,lse->de/dot_general | solution.py:48
  235.5 6.2 %fusion.76 = (bf16[8,384]{1,0:T(8,128)(2,1)S(1)}, f32[8,256]{1,0:T(8,128)S(1)}, f32[8,256]{1,0:T(8,128)S(1)}, bf16[8,384]{1,0:T(8,128)(2,1)S(1)}, f32[8,256,384]{2,1,0:T(8,128)S(1)}) fusion(bf16[8,256,384]{2,1,0:T(8,128)(2,1)S(1)} %copy-done, f32[8,256]{1,0:T(8,128)S(1)} %add_rsqrt_fusion.1, f32[8,256]{1,0:T(8,128)S(1)} %broadcast_multiply_fusion.5, ...), kind=kOutput, calls=%fused_computation.91 | convolution fusion | flops 1833949184 | bytes 10379264 | tf_op jit(solution)/shard_map/lse,de->lsd/dot_general | solution.py:176
  241.8 3.1 multiply_reduce_fusion.3
  247.0 4.8 %reduce-scatter.8.cloned.1.call-done = bf16[96,1152]{1,0:T(8,128)(2,1)} async-done(((bf16[384,1152]{1,0:T(8,128)(2,1)}), bf16[96,1152]{1,0:T(8,128)(2,1)}) %reduce-scatter.8.cloned.1.call-update) | async-done | bytes 221200 | tf_op jit(solution)/shard_map/reduce_scatter | solution.py:194
  251.9 28.1 %reduce-scatter.12.cloned.1.call-done = bf16[96,1536]{1,0:T(8,128)(2,1)} async-done(((bf16[384,1536]{1,0:T(8,128)(2,1)}), bf16[96,1536]{1,0:T(8,128)(2,1)}) %reduce-scatter.12.cloned.1.call-update) | async-done | bytes 294928 | tf_op jit(solution)/shard_map/reduce_scatter | solution.py:206
  280.0 28.5 %reduce-scatter.14.cloned.1.call-done = bf16[384,384]{1,0:T(8,128)(2,1)} async-done(((bf16[1536,384]{1,0:T(8,128)(2,1)}), bf16[384,384]{1,0:T(8,128)(2,1)}) %reduce-scatter.14.cloned.1.call-update) | async-done | bytes 294928 | tf_op jit(solution)/shard_map/reduce_scatter | solution.py:212
  308.5 32.0 %reduce-scatter.6.cloned.1.call-done = bf16[96,2304]{1,0:T(8,128)(2,1)} async-done(((bf16[384,2304]{1,0:T(8,128)(2,1)}), bf16[96,2304]{1,0:T(8,128)(2,1)}) %reduce-scatter.6.cloned.1.call-update) | async-done | bytes 442384 | tf_op jit(solution)/shard_map/reduce_scatter | solution.py:188
  345.4 10.5 %all-reduce.11 = (bf16[2304]{0:T(1024)(128)(2,1)S(1)}, bf16[768]{0:T(1024)(128)(2,1)S(1)}, bf16[384]{0:T(512)(128)(2,1)S(1)}, bf16[1536]{0:T(1024)(128)(2,1)S(1)}, bf16[384]{0:T(512)(128)(2,1)S(1)}) all-reduce(bf16[2304]{0:T(1024)(128)(2,1)S(1)} %reduce_sum.215, ...), channel_id=3, replica_groups=mesh['rep'=8,'shard'=4] {'shard'}, use_global_device_ids=true, to_apply=%region_24.25.clone | all-reduce | flops 5376 | bytes 21504
  356.4 22.2 %all-reduce.9 = (bf16[576]{0:T(1024)(128)(2,1)S(1)}, bf16[192]{0:T(256)(128)(2,1)S(1)}, bf16[96]{0:T(256)(128)(2,1)S(1)}, bf16[384]{0:T(512)(128)(2,1)S(1)}, bf16[96]{0:T(256)(128)(2,1)S(1)}) all-reduce(bf16[576]{0:T(1024)(128)(2,1)S(1)} %dynamic-slice.5, ...), channel_id=1, replica_groups=mesh['rep'=8,'shard'=4] {'rep'}, use_global_device_ids=true, to_apply=%region_25.26 | all-reduce | flops 1344 | bytes 5376 | tf_op jit(solution)/shard_map/psum | solution.py:221
  382.5 47.9 %all-reduce.15.cloned.1.call-done = (bf16[96,2304]{1,0:T(8,128)(2,1)}, bf16[96,1152]{1,0:T(8,128)(2,1)}, bf16[96,384]{1,0:T(8,128)(2,1)}, bf16[96,1536]{1,0:T(8,128)(2,1)}, bf16[384,384]{1,0:T(8,128)(2,1)}) async-done(((bf16[96,2304]{1,0:T(8,128)(2,1)}, bf16[96,1152]{1,0:T(8,128)(2,1)}, bf16[96,384]{1,0:T(8,128)(2,1)}, bf16[96,1536]{1,0:T(8,128)(2,1)}, bf16[384,384]{1,0:T(8,128)(2,1)}), ...) | async-done | bytes 1327120 | tf_op jit(solution)/shard_map/psum | solution.py:220
  (220 shorter events, 107.6 us)
Async XLA Ops:
  7.2 38.2 %copy-start.10 = (bf16[96,1152]{1,0:T(8,128)(2,1)S(1)}, bf16[96,1152]{1,0:T(8,128)(2,1)}, u32[]{:S(2)}) copy-start(bf16[96,1152]{1,0:T(8,128)(2,1)} %param.21) | copy-start | bytes 663556
  7.2 37.3 %copy-start = (bf16[8,256,384]{2,1,0:T(8,128)(2,1)S(1)}, bf16[8,256,384]{2,1,0:T(8,128)(2,1)}, u32[]{:S(2)}) copy-start(bf16[8,256,384]{2,1,0:T(8,128)(2,1)} %param.17) | copy-start | bytes 4718596
  7.2 53.4 %all-gather.5.cloned.1.call-start = ((), (), s32[]{:S(2)}) async-start(), calls=%async_computation.5 | async-start | bytes 2211840 | tf_op jit(solution)/shard_map/all_gather | solution.py:95
  7.9 95.7 %all-gather.7.cloned.1.call-start = ((), (), s32[]{:S(2)}) async-start(), calls=%async_computation.6 | async-start | bytes 1474560 | tf_op jit(solution)/shard_map/all_gather | solution.py:101
  8.7 106.0 %all-gather.9.cloned.1.call-start = ((), (), s32[]{:S(2)}) async-start(), calls=%async_computation.7 | async-start | bytes 1474560 | tf_op jit(solution)/shard_map/all_gather | solution.py:103
  8.7 36.7 %collective-permute-start = (bf16[1,96,1152]{2,1,0:T(8,128)(2,1)}, bf16[1,96,1152]{2,1,0:T(8,128)(2,1)S(1)}, u32[]{:S(2)}, u32[]{:S(2)}) collective-permute-start(bf16[1,96,1152]{2,1,0:T(8,128)(2,1)} %bitcast.183), channel_id=1, source_target_pairs={{0,1},{1,0},{2,3},{3,2},{4,5},{5,4},{6,7},{7,6},{8,9},{9,8},{10,11... | collective-permute-start | bytes 663560 | tf_op jit(solution)/shard_map/ppermute | solution.py:20
  9.4 237.6 %reduce-scatter.10.cloned.1.call-start = ((), (), s32[]{:S(2)}) async-start(), calls=%async_computation.10 | async-start | bytes 368640 | tf_op jit(solution)/shard_map/reduce_scatter | solution.py:200
  31.4 64.7 %copy-start.23 = (f32[384]{0:T(512)}, f32[384]{0:T(512)S(1)}, u32[]{:S(2)}) copy-start(f32[384]{0:T(512)S(1)} %convert_element_type.177) | copy-start | bytes 4612
  44.5 16.1 %copy-start.13 = (bf16[8,384]{1,0:T(8,128)(2,1)S(1)}, bf16[8,384]{1,0:T(8,128)(2,1)}, u32[]{:S(2)}) copy-start(bf16[8,384]{1,0:T(8,128)(2,1)} %param.18) | copy-start | bytes 18436
  45.5 14.9 %collective-permute-start.1 = (bf16[2,96,1152]{2,1,0:T(8,128)(2,1)S(1)}, bf16[2,96,1152]{2,1,0:T(8,128)(2,1)S(1)}, u32[]{:S(2)}, u32[]{:S(2)}) collective-permute-start(bf16[2,96,1152]{2,1,0:T(8,128)(2,1)S(1)} %pad_maximum_fusion.2), channel_id=1, source_target_pairs={{0,2},{1,3},{2,0},{3,1},{4,6},{5,7},{6,4},{7,5},{8,10},{9,11},{10,... | collective-permute-start | bytes 1327112 | tf_op jit(solution)/shard_map/ppermute | solution.py:20
  114.6 14.8 %copy-start.34 = (bf16[384,1536]{1,0:T(8,128)(2,1)S(1)}, bf16[384,1536]{1,0:T(8,128)(2,1)}, u32[]{:S(2)}) copy-start(bf16[384,1536]{1,0:T(8,128)(2,1)} %all-gather.7.cloned.1.call-done) | copy-start | bytes 3538948
  129.4 4.6 %copy-start.9 = (bf16[8,256,384]{2,1,0:T(8,128)(2,1)S(1)}, bf16[8,256,384]{2,1,0:T(8,128)(2,1)}, u32[]{:S(2)}) copy-start(bf16[8,256,384]{2,1,0:T(8,128)(2,1)} %param.29) | copy-start | bytes 4718596
  129.5 5.0 %copy-start.35 = (bf16[1536,384]{1,0:T(8,128)(2,1)S(1)}, bf16[1536,384]{1,0:T(8,128)(2,1)}, u32[]{:S(2)}) copy-start(bf16[1536,384]{1,0:T(8,128)(2,1)} %all-gather.9.cloned.1.call-done) | copy-start | bytes 3538948
  129.5 6.8 %copy-start.37 = (bf16[8,256,1536]{2,1,0:T(8,128)(2,1)S(1)}, bf16[8,256,1536]{2,1,0:T(8,128)(2,1)}, u32[]{:S(2)}) copy-start(bf16[8,256,1536]{2,1,0:T(8,128)(2,1)} %get-tuple-element.209) | copy-start | bytes 18874372
  203.0 5.5 %copy-start.18 = (f32[8,384]{1,0:T(8,128)S(1)}, f32[8,384]{1,0:T(8,128)}, u32[]{:S(2)}) copy-start(f32[8,384]{1,0:T(8,128)} %get-tuple-element.198) | copy-start | bytes 36868
  203.0 5.5 %copy-start.22 = (f32[8,256]{1,0:T(8,128)S(1)}, f32[8,256]{1,0:T(8,128)}, u32[]{:S(2)}) copy-start(f32[8,256]{1,0:T(8,128)} %add_rsqrt_fusion) | copy-start | bytes 24580
  203.0 5.5 %copy-start.25 = (f32[8,384]{1,0:T(8,128)S(1)}, f32[8,384]{1,0:T(8,128)}, u32[]{:S(2)}) copy-start(f32[8,384]{1,0:T(8,128)} %get-tuple-element.197) | copy-start | bytes 36868
  203.0 48.9 %reduce-scatter.8.cloned.1.call-start = ((), (), s32[]{:S(2)}) async-start(), calls=%async_computation.9 | async-start | bytes 1105920 | tf_op jit(solution)/shard_map/reduce_scatter | solution.py:194
  208.4 19.3 %copy-start.16 = (f32[8,384]{1,0:T(8,128)S(1)}, f32[8,384]{1,0:T(8,128)}, u32[]{:S(2)}) copy-start(f32[8,384]{1,0:T(8,128)} %get-tuple-element.196) | copy-start | bytes 36868
  208.4 71.6 %reduce-scatter.12.cloned.1.call-start = ((), (), s32[]{:S(2)}) async-start(), calls=%async_computation.11 | async-start | bytes 1474560 | tf_op jit(solution)/shard_map/reduce_scatter | solution.py:206
  216.2 92.3 %reduce-scatter.14.cloned.1.call-start = ((), (), s32[]{:S(2)}) async-start(), calls=%async_computation.12 | async-start | bytes 1474560 | tf_op jit(solution)/shard_map/reduce_scatter | solution.py:212
  235.4 6.3 %copy-start.24 = (f32[384]{0:T(512)S(1)}, f32[384]{0:T(512)}, u32[]{:S(2)}) copy-start(f32[384]{0:T(512)} %copy-done.23) | copy-start | bytes 4612
  235.4 105.1 %reduce-scatter.6.cloned.1.call-start = ((), (), s32[]{:S(2)}) async-start(), calls=%async_computation.8 | async-start | bytes 2211840 | tf_op jit(solution)/shard_map/reduce_scatter | solution.py:188
  235.5 6.3 %copy-start.4 = (f32[8,256,384]{2,1,0:T(8,128)S(1)}, f32[8,256,384]{2,1,0:T(8,128)}, u32[]{:S(2)}) copy-start(f32[8,256,384]{2,1,0:T(8,128)} %get-tuple-element.208) | copy-start | bytes 9437188
  235.5 6.3 %copy-start.5 = (f32[8,256,384]{2,1,0:T(8,128)S(1)}, f32[8,256,384]{2,1,0:T(8,128)}, u32[]{:S(2)}) copy-start(f32[8,256,384]{2,1,0:T(8,128)} %get-tuple-element.174) | copy-start | bytes 9437188
  246.9 98.5 %copy-start.30 = (bf16[384]{0:T(512)(128)(2,1)S(1)}, bf16[384]{0:T(512)(128)(2,1)}, u32[]{:S(2)}) copy-start(bf16[384]{0:T(512)(128)(2,1)} %get-tuple-element.172) | copy-start | bytes 2308
  246.9 98.5 %copy-start.31 = (bf16[384]{0:T(512)(128)(2,1)S(1)}, bf16[384]{0:T(512)(128)(2,1)}, u32[]{:S(2)}) copy-start(bf16[384]{0:T(512)(128)(2,1)} %get-tuple-element.191) | copy-start | bytes 2308
  246.9 98.5 %copy-start.32 = (bf16[1536]{0:T(1024)(128)(2,1)S(1)}, bf16[1536]{0:T(1024)(128)(2,1)}, u32[]{:S(2)}) copy-start(bf16[1536]{0:T(1024)(128)(2,1)} %get-tuple-element.212) | copy-start | bytes 9220
  247.0 134.4 %copy-start.6 = (bf16[384,2304]{1,0:T(8,128)(2,1)S(1)}, bf16[384,2304]{1,0:T(8,128)(2,1)}, u32[]{:S(2)}) copy-start(bf16[384,2304]{1,0:T(8,128)(2,1)} %all-gather.5.cloned.1.call-done) | copy-start | bytes 5308420
  247.0 183.5 %all-reduce.15.cloned.1.call-start = ((), (), s32[]{:S(2)}) async-start(), calls=%async_computation.13 | async-start | bytes 2654208 | tf_op jit(solution)/shard_map/psum | solution.py:220
  430.4 5.7 %copy-start.11 = (bf16[96,1152]{1,0:T(8,128)(2,1)S(1)}, bf16[96,1152]{1,0:T(8,128)(2,1)}, u32[]{:S(2)}) copy-start(bf16[96,1152]{1,0:T(8,128)(2,1)} %get-tuple-element.159) | copy-start | bytes 663556
  430.4 6.5 %copy-start.12 = (bf16[96,384]{1,0:T(8,128)(2,1)S(1)}, bf16[96,384]{1,0:T(8,128)(2,1)}, u32[]{:S(2)}) copy-start(bf16[96,384]{1,0:T(8,128)(2,1)} %get-tuple-element.160) | copy-start | bytes 221188
  (20 other events, 62.2 us)
Sparse Core Ops, SparseCore 0:
  9.6 23.6 all-gather.4
  34.9 19.9 all-gather.6
  56.4 17.1 all-gather.8
  203.1 21.7 reduce-scatter.9
  228.0 23.8 reduce-scatter.7
  254.3 25.6 reduce-scatter.11
  282.8 25.7 reduce-scatter.13
  311.1 29.3 reduce-scatter.5
  345.1 85.3 all-reduce.14
